TPU v7x, 256 devices: a whole 4x4x8 slice. The times are simulated.
256 devices in a mesh: section: 4 (over x_lo, core), expert: 64 (over x_hi, y, z).
Axes of the slice: x: 4 (x_hi: 2, x_lo: 2; x = x_hi * 2 + x_lo), y: 4, z: 8, core: 2. Of those that a mesh axis runs over, the one named last changes fastest.
Arguments:
- x_forward: bfloat16 [4, 512, 7168], P('section', 'expert'), may hold values from -6 to 6
- route_forward: int32 [4, 512, 2], P('section', 'expert'), may hold values from 0 to 7, all different within a row; in each aligned block of 8 rows (0 to 7, 8 to 15, ..., all dimensions but the last counted through in order) at most 3 rows name the same one
- gate_forward: float32 [4, 512, 2], P('section', 'expert'), may hold values from 0.2 to 1
- x_backward: bfloat16 [4, 512, 7168], P('section', 'expert'), may hold values from -6 to 6
- grad_output: bfloat16 [4, 512, 7168], P('section', 'expert'), may hold values from -6 to 6
- route_backward: int32 [4, 512, 2], P('section', 'expert'), may hold values from 0 to 7, all different within a row; in each aligned block of 8 rows (0 to 7, 8 to 15, ..., all dimensions but the last counted through in order) at most 3 rows name the same one
- gate_backward: float32 [4, 512, 2], P('section', 'expert'), may hold values from 0.2 to 1
- w_gate: bfloat16 [4, 7168, 16384], P('section', None, 'expert'), may hold values from -0.0625 to 0.0625
- w_up: bfloat16 [4, 7168, 16384], P('section', None, 'expert'), may hold values from -0.0625 to 0.0625
- w_down: bfloat16 [4, 16384, 7168], P('section', 'expert'), may hold values from -0.125 to 0.125
Outputs:
- forward_sent: bfloat16 [4, 512, 7168], P('section', 'expert')
- backward_sent: bfloat16 [4, 512, 7168], P('section', 'expert')
Inputs may be any that keep to these rules, and one draw needn't show every extreme that they name: `route_forward`: in each aligned block of 8 tokens a token names 2 different experts, no expert is named by more than 3 tokens of the block, a bound that some block reaches. `route_backward`: as for route_forward.
All inputs are finite; a program needn't handle non-finite values.
Results may differ from a plain program's by a relative error of at most 0.007.
Values may be sent and summed in bfloat16 or wider, within the bound.
A program may use at most 128 MiB of HBM per device.

v0:
```python
import jax
import jax.numpy as jnp
from jax import lax
from jax.sharding import PartitionSpec as P

GROUP = 8


def passed_along(block, axis, distance):
    devices = range(lax.axis_size(axis))
    route = [((i - distance) % len(devices), i) for i in devices]
    return lax.ppermute(block, axis, route)


def tables(route, gates, experts, cap):
    top = route.shape[-1]
    flat = route.reshape(-1)
    count = flat.shape[0]
    expert_hot = (flat[:, None] == jnp.arange(experts, dtype=jnp.int32)[None, :]).astype(jnp.int32)
    ranks = jnp.cumsum(expert_hot, axis=0) - 1
    slot = jnp.sum(ranks * expert_hot, axis=1)
    position = flat * cap + slot
    place_hot = (position[:, None] == jnp.arange(experts * cap, dtype=jnp.int32)[None, :]).astype(
        jnp.float32
    )
    owner = jnp.arange(count, dtype=jnp.int32) // top
    token_hot = (owner[:, None] == jnp.arange(count // top, dtype=jnp.int32)[None, :]).astype(
        jnp.float32
    )
    select = jnp.dot(place_hot.T, token_hot, precision=lax.Precision.HIGHEST)
    weights = jnp.dot(
        token_hot.T, place_hot * gates.reshape(-1)[:, None], precision=lax.Precision.HIGHEST
    )
    return (select, weights)


def on_device(
    x_forward,
    route_forward,
    gate_forward,
    x_backward,
    grad_output,
    route_backward,
    gate_backward,
    w_gate,
    w_up,
    w_down,
):
    devices = lax.axis_size("expert")
    experts = devices // GROUP
    tok_here = x_forward.shape[1]
    width = x_forward.shape[2]
    top = route_forward.shape[2]
    cap = min(tok_here, 3 * tok_here * top // (2 * experts))
    wg = w_gate[0]
    wu = w_up[0]
    wd = w_down[0]
    sel_f, wts_f = tables(route_forward[0], gate_forward[0], experts, cap)
    sel_b, wts_b = tables(route_backward[0], gate_backward[0], experts, cap)

    def pack(select, rows):
        send = jnp.dot(
            select.astype(jnp.bfloat16), rows, preferred_element_type=jnp.float32
        ).astype(jnp.bfloat16)
        send = jnp.broadcast_to(send.reshape(experts, 1, cap, width), (experts, GROUP, cap, width))
        return send.reshape(devices, cap, width)

    def spread(weights, result, base):
        total = jnp.sum(result.astype(jnp.float32).reshape(experts, GROUP, cap, width), axis=1)
        summed = jnp.dot(
            weights, total.reshape(experts * cap, width), precision=lax.Precision.HIGHEST
        )
        return (base.astype(jnp.float32) + summed).astype(jnp.bfloat16)

    send_f = pack(sel_f, x_forward[0])
    send_x = pack(sel_b, x_backward[0])
    send_dy = pack(sel_b, grad_output[0])
    recv = lax.all_to_all(send_f, "expert", split_axis=0, concat_axis=0, tiled=True)
    rows = recv.reshape(-1, width)
    a_pre = jnp.dot(rows, wg, preferred_element_type=jnp.float32)
    b_pre = jnp.dot(rows, wu, preferred_element_type=jnp.float32)
    hidden = (jax.nn.silu(a_pre) * b_pre).astype(jnp.bfloat16)
    part = jnp.dot(hidden, wd, preferred_element_type=jnp.float32).astype(jnp.bfloat16)
    result_f = lax.all_to_all(
        part.reshape(recv.shape), "expert", split_axis=0, concat_axis=0, tiled=True
    )
    recv_x = lax.all_to_all(send_x, "expert", split_axis=0, concat_axis=0, tiled=True)
    rows = recv_x.reshape(-1, width)
    grads = lax.all_to_all(send_dy, "expert", split_axis=0, concat_axis=0, tiled=True).reshape(
        -1, width
    )
    a_pre = jnp.dot(rows, wg, preferred_element_type=jnp.float32)
    b_pre = jnp.dot(rows, wu, preferred_element_type=jnp.float32)
    d_hidden = lax.dot_general(
        grads, wd, (((1,), (1,)), ((), ())), preferred_element_type=jnp.float32
    )
    sig = jax.nn.sigmoid(a_pre)
    d_a = (d_hidden * b_pre * sig * (1.0 + a_pre * (1.0 - sig))).astype(jnp.bfloat16)
    d_b = (d_hidden * a_pre * sig).astype(jnp.bfloat16)
    back = lax.dot_general(d_a, wg, (((1,), (1,)), ((), ())), preferred_element_type=jnp.float32)
    back = back + lax.dot_general(
        d_b, wu, (((1,), (1,)), ((), ())), preferred_element_type=jnp.float32
    )
    result_b = lax.all_to_all(
        back.astype(jnp.bfloat16).reshape(recv_x.shape),
        "expert",
        split_axis=0,
        concat_axis=0,
        tiled=True,
    )
    out = spread(wts_f, result_f, x_forward[0])
    grad = spread(wts_b, result_b, grad_output[0])
    forward_sent = passed_along(out[None], "section", 1)
    backward_sent = passed_along(grad[None], "section", -1)
    return (forward_sent, backward_sent)


def solution(mesh):
    in_specs = (
        P("section", "expert", None),
        P("section", "expert", None),
        P("section", "expert", None),
        P("section", "expert", None),
        P("section", "expert", None),
        P("section", "expert", None),
        P("section", "expert", None),
        P("section", None, "expert"),
        P("section", None, "expert"),
        P("section", "expert", None),
    )
    out_specs = (P("section", "expert", None), P("section", "expert", None))
    return jax.shard_map(
        on_device, mesh=mesh, in_specs=in_specs, out_specs=out_specs, check_vma=False
    )
```

profile of v0, /device:TPU:1, one launch (start us, length us, event | category | flops | bytes accessed | tf_op | source)
XLA Modules:
  0.0 494.7 jit_solution(12275337424624484415)
XLA Ops:
  0.6 0.8 copy.16
  1.6 0.2 select_reduce_fusion.1
  1.8 0.3 convolution_convert_fusion.4
  2.1 1.1 convolution_convert_fusion.3
  3.2 0.2 broadcast_in_dim.16
  3.4 2.9 broadcast_in_dim.17
  6.3 15.5 %all-to-all-start = ((bf16[64,3,7168]{2,1,0:T(4,128)(2,1)}), bf16[64,3,7168]{2,1,0:T(4,128)(2,1)}, u32[]{:S(2)}, u32[]{:S(2)}) async-start(bf16[64,3,7168]{2,1,0:T(4,128)(2,1)} %bitcast.71), calls=%async_computation | async-start | bytes 7340032 | tf_op jit(solution)/shard_map/all_to_all | solution.py:78
  22.1 0.2 select_reduce_fusion
  22.3 0.3 convolution_convert_fusion.5
  22.5 0.3 convolution_convert_fusion.2
  22.8 0.2 broadcast_in_dim.19
  23.1 80.5 %all-to-all-done = bf16[64,3,7168]{2,1,0:T(4,128)(2,1)} async-done(((bf16[64,3,7168]{2,1,0:T(4,128)(2,1)}), bf16[64,3,7168]{2,1,0:T(4,128)(2,1)}, u32[]{:S(2)}, u32[]{:S(2)}) %all-to-all-start) | async-done | bytes 2752544 | tf_op jit(solution)/shard_map/all_to_all | solution.py:78
  103.5 3.0 broadcast_in_dim.20
  106.6 11.1 %all-to-all-start.2 = ((bf16[64,3,7168]{2,1,0:T(4,128)(2,1)}), bf16[64,3,7168]{2,1,0:T(4,128)(2,1)}, u32[]{:S(2)}, u32[]{:S(2)}) async-start(bf16[64,3,7168]{2,1,0:T(4,128)(2,1)} %bitcast.73), calls=%async_computation.2 | async-start | bytes 7340032 | tf_op jit(solution)/shard_map/all_to_all | solution.py:89
  117.7 0.3 convolution_convert_fusion.1
  118.0 0.2 broadcast_in_dim.42
  118.2 81.3 %all-to-all-done.2 = bf16[64,3,7168]{2,1,0:T(4,128)(2,1)} async-done(((bf16[64,3,7168]{2,1,0:T(4,128)(2,1)}), bf16[64,3,7168]{2,1,0:T(4,128)(2,1)}, u32[]{:S(2)}, u32[]{:S(2)}) %all-to-all-start.2) | async-done | bytes 2752544 | tf_op jit(solution)/shard_map/all_to_all | solution.py:89
  199.4 3.0 broadcast_in_dim.43
  202.5 11.1 %all-to-all-start.3 = ((bf16[64,3,7168]{2,1,0:T(4,128)(2,1)}), bf16[64,3,7168]{2,1,0:T(4,128)(2,1)}, u32[]{:S(2)}, u32[]{:S(2)}) async-start(bf16[64,3,7168]{2,1,0:T(4,128)(2,1)} %bitcast.72), calls=%async_computation.3 | async-start | bytes 7340032 | tf_op jit(solution)/shard_map/all_to_all | solution.py:87
  213.5 5.7 %reshape.86 = bf16[192,7168]{1,0:T(8,128)(2,1)S(1)} reshape(bf16[64,3,7168]{2,1,0:T(4,128)(2,1)} %all-to-all-done) | data formatting | bytes 5505024 | tf_op jit(solution)/shard_map/reshape | solution.py:79
  219.2 2.9 fusion.17
  222.2 7.7 %convolution_convert_fusion = bf16[192,7168]{1,0:T(8,128)(2,1)} fusion(bf16[1,256,7168]{2,1,0:T(8,128)(2,1)} %param.19, bf16[192,7168]{1,0:T(8,128)(2,1)S(1)} %reshape.86, bf16[1,7168,256]{2,1,0:T(8,128)(2,1)} %param.18, f32[192,256]{1,0:T(8,128)S(1)} %fusion.17), kind=kOutput, calls=%fused_computation.2 | convolution fusion | flops 1410957312 | bytes 13041664 | tf_op jit(solution)/shard_map/dot_general | solution.py:83
  229.9 6.8 %reshape.87 = bf16[64,3,7168]{2,1,0:T(4,128)(2,1)} reshape(bf16[192,7168]{1,0:T(8,128)(2,1)} %convolution_convert_fusion) | data formatting | bytes 5505024 | tf_op jit(solution)/shard_map/reshape | solution.py:85
  236.7 58.7 %all-to-all-done.3 = bf16[64,3,7168]{2,1,0:T(4,128)(2,1)} async-done(((bf16[64,3,7168]{2,1,0:T(4,128)(2,1)}), bf16[64,3,7168]{2,1,0:T(4,128)(2,1)}, u32[]{:S(2)}, u32[]{:S(2)}) %all-to-all-start.3) | async-done | bytes 2752544 | tf_op jit(solution)/shard_map/all_to_all | solution.py:87
  295.4 11.1 %all-to-all-start.1 = ((bf16[64,3,7168]{2,1,0:T(4,128)(2,1)}), bf16[64,3,7168]{2,1,0:T(4,128)(2,1)}, u32[]{:S(2)}, u32[]{:S(2)}) async-start(bf16[64,3,7168]{2,1,0:T(4,128)(2,1)} %reshape.87), calls=%async_computation.1 | async-start | bytes 7340032 | tf_op jit(solution)/shard_map/all_to_all | solution.py:84
  306.5 7.1 %reshape.92 = bf16[192,7168]{1,0:T(8,128)(2,1)} reshape(bf16[64,3,7168]{2,1,0:T(4,128)(2,1)} %all-to-all-done.2) | data formatting | bytes 5505024 | tf_op jit(solution)/shard_map/reshape | solution.py:89
  313.6 5.7 %reshape.94 = bf16[192,7168]{1,0:T(8,128)(2,1)S(1)} reshape(bf16[64,3,7168]{2,1,0:T(4,128)(2,1)} %all-to-all-done.3) | data formatting | bytes 5505024 | tf_op jit(solution)/shard_map/reshape | solution.py:88
  319.3 4.4 fusion.5
  323.7 0.9 fusion.15
  324.6 8.9 %fusion.13 = f32[192,7168]{1,0:T(8,128)} fusion(bf16[1,7168,256]{2,1,0:T(8,128)(2,1)} %param.17, f32[192,256]{1,0:T(8,128)S(1)} %fusion.5, bf16[192,7168]{1,0:T(8,128)(2,1)S(1)} %reshape.94, bf16[1,7168,256]{2,1,0:T(8,128)(2,1)} %param.18, f32[192,256]{1,0:T(8,128)S(1)} %fusion.15), kind=kOutput, calls=%fused_computation.22 | convolution fusion | flops 1409777664 | bytes 15990784 | tf_op jit(solution)/shard_map/dot_general | solution.py:100
  333.5 5.0 %fusion = bf16[192,7168]{1,0:T(8,128)(2,1)S(1)} fusion(f32[192,7168]{1,0:T(8,128)} %fusion.13, bf16[1,7168,256]{2,1,0:T(8,128)(2,1)} %param.18, f32[192,256]{1,0:T(8,128)S(1)} %fusion.5, f32[192,256]{1,0:T(8,128)S(1)} %fusion.15), kind=kOutput, calls=%fused_computation.1 | convolution fusion | flops 707690496 | bytes 12320768 | tf_op jit(solution)/shard_map/dot_general | solution.py:101
  338.5 4.1 reshape.95
  342.7 45.7 %all-to-all-done.1 = bf16[64,3,7168]{2,1,0:T(4,128)(2,1)} async-done(((bf16[64,3,7168]{2,1,0:T(4,128)(2,1)}), bf16[64,3,7168]{2,1,0:T(4,128)(2,1)}, u32[]{:S(2)}, u32[]{:S(2)}) %all-to-all-start.1) | async-done | bytes 2752544 | tf_op jit(solution)/shard_map/all_to_all | solution.py:84
  388.3 11.0 %all-to-all-start.4 = ((bf16[64,3,7168]{2,1,0:T(4,128)(2,1)}), bf16[64,3,7168]{2,1,0:T(4,128)(2,1)}, u32[]{:S(2)}, u32[]{:S(2)}) async-start(bf16[64,3,7168]{2,1,0:T(4,128)(2,1)} %reshape.95), calls=%async_computation.4 | async-start | bytes 7340032 | tf_op jit(solution)/shard_map/all_to_all | solution.py:104
  399.7 0.3 fusion.58
  400.0 0.3 fusion.55
  400.2 3.9 convert_reduce_fusion.1
  404.1 0.3 reshape.90
  404.5 0.5 fusion.4
  404.9 1.3 collective-permute-start
  406.2 75.0 %all-to-all-done.4 = bf16[64,3,7168]{2,1,0:T(4,128)(2,1)} async-done(((bf16[64,3,7168]{2,1,0:T(4,128)(2,1)}), bf16[64,3,7168]{2,1,0:T(4,128)(2,1)}, u32[]{:S(2)}, u32[]{:S(2)}) %all-to-all-start.4) | async-done | bytes 2752544 | tf_op jit(solution)/shard_map/all_to_all | solution.py:104
  481.3 3.8 convert_reduce_fusion
  485.1 0.3 reshape.98
  485.5 0.5 fusion.3
  485.9 4.8 collective-permute-start.1
  490.7 2.7 collective-permute-done.1
  493.4 0.6 copy.22
  494.0 0.6 copy.23
  (30 shorter events, 0.9 us)
Async XLA Ops:
  0.6 117.0 %copy-start = (bf16[1,8,7168]{2,1,0:T(8,128)(2,1)S(1)}, bf16[1,8,7168]{2,1,0:T(8,128)(2,1)}, u32[]{:S(2)}) copy-start(bf16[1,8,7168]{2,1,0:T(8,128)(2,1)} %param.13) | copy-start | bytes 344068
  6.3 15.5 %copy-start.5 = (s32[1,8,2]{1,2,0:T(2,128)S(1)}, s32[1,8,2]{1,2,0:T(2,128)}, u32[]{:S(2)}) copy-start(s32[1,8,2]{1,2,0:T(2,128)} %param.15) | copy-start | bytes 196
  6.3 16.2 %copy-start.4 = (bf16[1,8,7168]{2,1,0:T(8,128)(2,1)S(1)}, bf16[1,8,7168]{2,1,0:T(8,128)(2,1)}, u32[]{:S(2)}) copy-start(bf16[1,8,7168]{2,1,0:T(8,128)(2,1)} %param.14) | copy-start | bytes 344068
  6.3 97.2 %all-to-all-start = ((bf16[64,3,7168]{2,1,0:T(4,128)(2,1)}), bf16[64,3,7168]{2,1,0:T(4,128)(2,1)}, u32[]{:S(2)}, u32[]{:S(2)}) async-start(bf16[64,3,7168]{2,1,0:T(4,128)(2,1)} %bitcast.71), calls=%async_computation | async-start | bytes 7340032 | tf_op jit(solution)/shard_map/all_to_all | solution.py:78
  106.6 92.9 %all-to-all-start.2 = ((bf16[64,3,7168]{2,1,0:T(4,128)(2,1)}), bf16[64,3,7168]{2,1,0:T(4,128)(2,1)}, u32[]{:S(2)}, u32[]{:S(2)}) async-start(bf16[64,3,7168]{2,1,0:T(4,128)(2,1)} %bitcast.73), calls=%async_computation.2 | async-start | bytes 7340032 | tf_op jit(solution)/shard_map/all_to_all | solution.py:89
  202.5 92.9 %all-to-all-start.3 = ((bf16[64,3,7168]{2,1,0:T(4,128)(2,1)}), bf16[64,3,7168]{2,1,0:T(4,128)(2,1)}, u32[]{:S(2)}, u32[]{:S(2)}) async-start(bf16[64,3,7168]{2,1,0:T(4,128)(2,1)} %bitcast.72), calls=%async_computation.3 | async-start | bytes 7340032 | tf_op jit(solution)/shard_map/all_to_all | solution.py:87
  295.4 93.0 %all-to-all-start.1 = ((bf16[64,3,7168]{2,1,0:T(4,128)(2,1)}), bf16[64,3,7168]{2,1,0:T(4,128)(2,1)}, u32[]{:S(2)}, u32[]{:S(2)}) async-start(bf16[64,3,7168]{2,1,0:T(4,128)(2,1)} %reshape.87), calls=%async_computation.1 | async-start | bytes 7340032 | tf_op jit(solution)/shard_map/all_to_all | solution.py:84
  319.2 4.4 copy-start.2
  342.7 56.7 %copy-start.6 = (f32[1,8,2]{1,2,0:T(2,128)S(1)}, f32[1,8,2]{1,2,0:T(2,128)}, u32[]{:S(2)}) copy-start(f32[1,8,2]{1,2,0:T(2,128)} %param.12) | copy-start | bytes 196
  342.7 56.9 %copy-start.7 = (f32[1,8,2]{1,2,0:T(2,128)S(1)}, f32[1,8,2]{1,2,0:T(2,128)}, u32[]{:S(2)}) copy-start(f32[1,8,2]{1,2,0:T(2,128)} %param.16) | copy-start | bytes 196
  388.3 92.9 %all-to-all-start.4 = ((bf16[64,3,7168]{2,1,0:T(4,128)(2,1)}), bf16[64,3,7168]{2,1,0:T(4,128)(2,1)}, u32[]{:S(2)}, u32[]{:S(2)}) async-start(bf16[64,3,7168]{2,1,0:T(4,128)(2,1)} %reshape.95), calls=%async_computation.4 | async-start | bytes 7340032 | tf_op jit(solution)/shard_map/all_to_all | solution.py:104
  399.4 5.1 %copy-start.3 = (bf16[1,8,7168]{2,1,0:T(8,128)(2,1)S(1)}, bf16[1,8,7168]{2,1,0:T(8,128)(2,1)}, u32[]{:S(2)}) copy-start(bf16[1,8,7168]{2,1,0:T(8,128)(2,1)} %param.10) | copy-start | bytes 344068
  404.5 90.2 %copy-start.1 = (bf16[1,8,7168]{2,1,0:T(8,128)(2,1)S(1)}, bf16[1,8,7168]{2,1,0:T(8,128)(2,1)}, u32[]{:S(2)}) copy-start(bf16[1,8,7168]{2,1,0:T(8,128)(2,1)} %param.13) | copy-start | bytes 344068
  404.9 85.8 %collective-permute-start = (bf16[1,8,7168]{2,1,0:T(8,128)(2,1)S(1)}, bf16[1,8,7168]{2,1,0:T(8,128)(2,1)S(1)}, u32[]{:S(2)}, u32[]{:S(2)}) collective-permute-start(bf16[1,8,7168]{2,1,0:T(8,128)(2,1)S(1)} %fusion.4), channel_id=1, source_target_pairs={{192,0},{0,64},{64,128},{128,192},{193,1},{1,65},{65,129},{129,193... | collective-permute-start | bytes 344072 | tf_op jit(solution)/shard_map/ppermute | solution.py:12
  485.9 7.4 %collective-permute-start.1 = (bf16[1,8,7168]{2,1,0:T(8,128)(2,1)S(1)}, bf16[1,8,7168]{2,1,0:T(8,128)(2,1)S(1)}, u32[]{:S(2)}, u32[]{:S(2)}) collective-permute-start(bf16[1,8,7168]{2,1,0:T(8,128)(2,1)S(1)} %fusion.3), channel_id=1, source_target_pairs={{64,0},{128,64},{192,128},{0,192},{65,1},{129,65},{193,129},{1,193... | collective-permute-start | bytes 344072 | tf_op jit(solution)/shard_map/ppermute | solution.py:12
where the time goes:
time: 496 us; the launch traced here: 495 us
  waiting for transfers between devices  344 us (69%)
  starting transfers between devices  65.8 us (13%)
  local copies, waits for them, and re-layouts  42.3 us (9%)
  matrix products  33.5 us (7%)
  other arithmetic  8.3 us (2%)
    all_to_all x1, waiting for transfers between devices, on_device(): lax.all_to_all(send_dy, 'expert', split_axis=0, concat_axis=0, tiled=True)  81.3 us
    all_to_all x1, waiting for transfers between devices, on_device(): lax.all_to_all(send_f, 'expert', split_axis=0, concat_axis=0, tiled=True)  80.5 us
    all_to_all x1, waiting for transfers between devices, on_device(): lax.all_to_all(back.astype(jnp.bfloat16).reshape(recv_x.shape), 'expert',...  75 us
    all_to_all x1, waiting for transfers between devices, on_device(): lax.all_to_all(send_x, 'expert', split_axis=0, concat_axis=0, tiled=True)  58.7 us
    all_to_all x1, waiting for transfers between devices, on_device(): lax.all_to_all(part.reshape(recv.shape), 'expert', split_axis=0, concat_a...  45.7 us
    all_to_all x1, starting transfers between devices, on_device(): lax.all_to_all(send_f, 'expert', split_axis=0, concat_axis=0, tiled=True)  15.5 us
    all_to_all x1, starting transfers between devices, on_device(): lax.all_to_all(send_x, 'expert', split_axis=0, concat_axis=0, tiled=True)  11.1 us
    all_to_all x1, starting transfers between devices, on_device(): lax.all_to_all(send_dy, 'expert', split_axis=0, concat_axis=0, tiled=True)  11.1 us
  transfers between devices with their start and end apart: 7, of which 6 were waited for; matrix products, arithmetic and copies ran while one was open for 14% of the time, Pallas kernels for 0%

commit v1 on v0

--- a/solution.py
+++ b/solution.py
@@ -58,37 +58,50 @@
     sel_f, wts_f = tables(route_forward[0], gate_forward[0], experts, cap)
     sel_b, wts_b = tables(route_backward[0], gate_backward[0], experts, cap)
 
+    plane = [[e * GROUP + m for e in range(experts)] for m in range(GROUP)]
+    line = [[e * GROUP + m for m in range(GROUP)] for e in range(experts)]
+
     def pack(select, rows):
         send = jnp.dot(
             select.astype(jnp.bfloat16), rows, preferred_element_type=jnp.float32
         ).astype(jnp.bfloat16)
-        send = jnp.broadcast_to(send.reshape(experts, 1, cap, width), (experts, GROUP, cap, width))
-        return send.reshape(devices, cap, width)
+        return send.reshape(experts, cap, width)
+
+    def deliver(send):
+        here = lax.all_to_all(
+            send, "expert", split_axis=0, concat_axis=0, axis_index_groups=plane, tiled=True
+        )
+        flat = here.reshape(experts * cap, -1)
+        return lax.all_gather(flat, "expert", axis=0, axis_index_groups=line, tiled=True)
+
+    def give_back(part):
+        summed = lax.psum_scatter(
+            part, "expert", scatter_dimension=0, axis_index_groups=line, tiled=True
+        )
+        return lax.all_to_all(
+            summed.reshape(experts, cap, width),
+            "expert",
+            split_axis=0,
+            concat_axis=0,
+            axis_index_groups=plane,
+            tiled=True,
+        )
 
     def spread(weights, result, base):
-        total = jnp.sum(result.astype(jnp.float32).reshape(experts, GROUP, cap, width), axis=1)
-        summed = jnp.dot(
-            weights, total.reshape(experts * cap, width), precision=lax.Precision.HIGHEST
-        )
+        total = result.astype(jnp.float32).reshape(experts * cap, width)
+        summed = jnp.dot(weights, total, precision=lax.Precision.HIGHEST)
         return (base.astype(jnp.float32) + summed).astype(jnp.bfloat16)
 
-    send_f = pack(sel_f, x_forward[0])
-    send_x = pack(sel_b, x_backward[0])
-    send_dy = pack(sel_b, grad_output[0])
-    recv = lax.all_to_all(send_f, "expert", split_axis=0, concat_axis=0, tiled=True)
-    rows = recv.reshape(-1, width)
+    rows = deliver(pack(sel_f, x_forward[0]))
     a_pre = jnp.dot(rows, wg, preferred_element_type=jnp.float32)
     b_pre = jnp.dot(rows, wu, preferred_element_type=jnp.float32)
     hidden = (jax.nn.silu(a_pre) * b_pre).astype(jnp.bfloat16)
     part = jnp.dot(hidden, wd, preferred_element_type=jnp.float32).astype(jnp.bfloat16)
-    result_f = lax.all_to_all(
-        part.reshape(recv.shape), "expert", split_axis=0, concat_axis=0, tiled=True
-    )
-    recv_x = lax.all_to_all(send_x, "expert", split_axis=0, concat_axis=0, tiled=True)
-    rows = recv_x.reshape(-1, width)
-    grads = lax.all_to_all(send_dy, "expert", split_axis=0, concat_axis=0, tiled=True).reshape(
-        -1, width
-    )
+    result_f = give_back(part)
+    both = jnp.concatenate([pack(sel_b, x_backward[0]), pack(sel_b, grad_output[0])], axis=2)
+    both = deliver(both)
+    rows = both[:, :width]
+    grads = both[:, width:]
     a_pre = jnp.dot(rows, wg, preferred_element_type=jnp.float32)
     b_pre = jnp.dot(rows, wu, preferred_element_type=jnp.float32)
     d_hidden = lax.dot_general(
@@ -101,13 +114,7 @@
     back = back + lax.dot_general(
         d_b, wu, (((1,), (1,)), ((), ())), preferred_element_type=jnp.float32
     )
-    result_b = lax.all_to_all(
-        back.astype(jnp.bfloat16).reshape(recv_x.shape),
-        "expert",
-        split_axis=0,
-        concat_axis=0,
-        tiled=True,
-    )
+    result_b = give_back(back.astype(jnp.bfloat16))
     out = spread(wts_f, result_f, x_forward[0])
     grad = spread(wts_b, result_b, grad_output[0])
     forward_sent = passed_along(out[None], "section", 1)

time: 496 us -> 262 us (0.53)
  waiting for transfers between devices: 344 us -> 139 us
  starting transfers between devices: 65.8 us -> 24.6 us
  blocking collectives: 0 us -> 33.4 us
  local copies, waits for them, and re-layouts: 42.3 us -> 11.1 us
  between operations: 0.89 us -> 13.9 us
  other arithmetic: 8.3 us -> 1.03 us
  matrix products: 33.5 us -> 38.6 us
    all_to_all x5 -> x2, waiting for transfers between devices: 341 us -> 2.3 us  [give_back(): lax.all_to_all(summed.reshape(experts, cap, width), 'expert', split_axis=...]
    all_gather x0 -> x2, waiting for transfers between devices: none -> 77.7 us  [deliver(): lax.all_gather(flat, 'expert', axis=0, axis_index_groups=line, tiled=True)]
    reduce_scatter x0 -> x2, waiting for transfers between devices: none -> 56.3 us  [give_back(): lax.psum_scatter(part, 'expert', scatter_dimension=0, axis_index_groups=l...]
    all_to_all x5 -> x2, starting transfers between devices: 59.7 us -> 12.9 us  [give_back(): lax.all_to_all(summed.reshape(experts, cap, width), 'expert', split_axis=...]
    all_to_all x0 -> x2, blocking collectives: none -> 33.4 us  [deliver(): lax.all_to_all(send, 'expert', split_axis=0, concat_axis=0, axis_index_gr...]
    reshape x7 -> x9, local copies, waits for them, and re-layouts: 30.1 us -> 7.69 us  [the longest x2 3.92 us: give_back(): summed.reshape(experts, cap, width)]
    broadcast_in_dim x6 -> x0, local copies, waits for them, and re-layouts: 9.57 us -> none  [pack(): jnp.broadcast_to(send.reshape(experts, 1, cap, width), (experts, GROUP, c...]
    reduce_sum x2 -> x0, other arithmetic: 7.7 us -> none  [spread(): jnp.sum(result.astype(jnp.float32).reshape(experts, GROUP, cap, width), a...]
  transfers between devices with their start and end apart: 7 -> 8, of which waited for: 6 -> 6; matrix products, arithmetic and copies ran while one was open for 14% -> 17% of each run, Pallas kernels for 0% -> 0%
where the time goes in v1:
time: 262 us
  waiting for transfers between devices  139 us (53%)
  matrix products  38.6 us (15%)
  blocking collectives  33.4 us (13%)
  starting transfers between devices  24.6 us (9%)
  between operations  13.9 us (5%)
  local copies, waits for them, and re-layouts  11.1 us (4%)
    all_gather x2, waiting for transfers between devices, deliver(): lax.all_gather(flat, 'expert', axis=0, axis_index_groups=line, tiled=True)  77.7 us
    reduce_scatter x2, waiting for transfers between devices, give_back(): lax.psum_scatter(part, 'expert', scatter_dimension=0, axis_index_groups=l...  56.3 us
    all_to_all x2, blocking collectives, deliver(): lax.all_to_all(send, 'expert', split_axis=0, concat_axis=0, axis_index_gr...  33.4 us
    all_to_all x2, starting transfers between devices, give_back(): lax.all_to_all(summed.reshape(experts, cap, width), 'expert', split_axis=...  12.9 us
    ppermute x2, starting transfers between devices, passed_along(): return lax.ppermute(block, axis, route)  11.6 us
    dot_general x1, matrix products, on_device(): lax.dot_general(d_a, wg, (((1,), (1,)), ((), ())), preferred_element_type...  9.76 us
    dot_general x1, matrix products, on_device(): jnp.dot(hidden, wd, preferred_element_type=jnp.float32).astype(jnp.bfloat16)  7.88 us
    dot_general x2, matrix products, on_device(): a_pre = jnp.dot(rows, wg, preferred_element_type=jnp.float32)  7.79 us
  transfers between devices with their start and end apart: 8, of which 6 were waited for; matrix products, arithmetic and copies ran while one was open for 17% of the time, Pallas kernels for 0%

profile of v1, /device:TPU:1, one launch (start us, length us, event | category | flops | bytes accessed | tf_op | source)
XLA Modules:
  0.0 262.0 jit_solution(11307936170687325149)
XLA Ops:
  7.2 0.8 copy.16
  8.0 0.1 reshape_squeeze.6
  8.2 0.2 select_reduce_fusion.1
  8.4 0.3 convolution_convert_fusion.4
  8.7 1.1 convolution_convert_fusion.3
  9.8 0.2 reshape.64
  10.0 16.8 %all_to_all.20 = bf16[8,3,7168]{2,1,0:T(4,128)(2,1)S(1)} all-to-all(bf16[8,3,7168]{2,1,0:T(4,128)(2,1)S(1)} %reshape.64), channel_id=1, replica_groups={{0,8,16,24,32,40,48,56},{1,9,17,25,33,41,49,57},{2,10,18,26,34,42,50,58..., dimensions={0} | all-to-all | bytes 688128 | tf_op jit(solution)/shard_map/all_to_all | solution.py:71
  26.8 1.1 reshape.65
  27.9 0.8 copy.18
  28.7 0.1 reshape_squeeze.7
  28.9 0.2 select_reduce_fusion
  29.1 0.3 convolution_convert_fusion.5
  29.3 0.3 convolution_convert_fusion.2
  29.6 0.2 reshape.68
  29.8 0.3 convolution_convert_fusion.1
  30.1 0.2 reshape.69
  30.4 0.4 pad_maximum_fusion
  30.8 16.6 %all_to_all.21 = bf16[8,3,14336]{2,1,0:T(4,128)(2,1)S(1)} all-to-all(bf16[8,3,14336]{2,1,0:T(4,128)(2,1)S(1)} %pad_maximum_fusion), channel_id=1, replica_groups={{0,8,16,24,32,40,48,56},{1,9,17,25,33,41,49,57},{2,10,18,26,34,42,50,58..., dimensions={0} | all-to-all | bytes 1376256 | tf_op jit(solution)/shard_map/all_to_all | solution.py:71
  47.4 1.5 reshape.70
  49.0 19.6 %all-gather.3.cloned.1.call-done = bf16[192,7168]{1,0:T(8,128)(2,1)} async-done(((bf16[24,7168]{1,0:T(8,128)(2,1)}), bf16[192,7168]{1,0:T(8,128)(2,1)}) %all-gather.3.cloned.1.call-update) | async-done | bytes 2752528 | tf_op jit(solution)/shard_map/all_gather | solution.py:75
  68.5 3.9 %fusion.17 = f32[192,256]{1,0:T(8,128)S(1)} fusion(bf16[192,7168]{1,0:T(8,128)(2,1)} %all-gather.3.cloned.1.call-done, bf16[1,7168,256]{2,1,0:T(8,128)(2,1)} %param.17), kind=kOutput, calls=%fused_computation.24 | convolution fusion | flops 704643072 | bytes 6619136 | tf_op jit(solution)/shard_map/dot_general | solution.py:96
  72.4 7.9 %convolution_convert_fusion = bf16[192,7168]{1,0:T(8,128)(2,1)} fusion(bf16[1,256,7168]{2,1,0:T(8,128)(2,1)} %param.19, bf16[192,7168]{1,0:T(8,128)(2,1)S(1)} %copy-done.1, bf16[1,7168,256]{2,1,0:T(8,128)(2,1)} %param.18, f32[192,256]{1,0:T(8,128)S(1)} %fusion.17), kind=kOutput, calls=%fused_computation.2 | convolution fusion | flops 1410957312 | bytes 13041664 | tf_op jit(solution)/shard_map/dot_general | solution.py:99
  80.4 58.2 %all-gather.5.cloned.1.call-done = bf16[192,14336]{1,0:T(8,128)(2,1)} async-done(((bf16[24,14336]{1,0:T(8,128)(2,1)}), bf16[192,14336]{1,0:T(8,128)(2,1)}) %all-gather.5.cloned.1.call-update) | async-done | bytes 5505040 | tf_op jit(solution)/shard_map/all_gather | solution.py:75
  138.6 3.9 %fusion.15 = f32[192,256]{1,0:T(8,128)S(1)} fusion(bf16[1,7168,256]{2,1,0:T(8,128)(2,1)} %param.17, bf16[192,14336]{1,0:T(8,128)(2,1)} %all-gather.5.cloned.1.call-done), kind=kOutput, calls=%fused_computation.22 | convolution fusion | flops 704643072 | bytes 6619136 | tf_op jit(solution)/shard_map/dot_general | solution.py:105
  142.5 3.1 %fusion.5 = f32[192,256]{1,0:T(8,128)S(1)} fusion(bf16[1,256,7168]{2,1,0:T(8,128)(2,1)S(1)} %copy-done.2, bf16[192,14336]{1,0:T(8,128)(2,1)} %all-gather.5.cloned.1.call-done), kind=kOutput, calls=%fused_computation.12 | convolution fusion | flops 704643072 | bytes 6619136 | tf_op jit(solution)/shard_map/dot_general | solution.py:107
  145.6 9.8 %fusion.13 = f32[192,7168]{1,0:T(8,128)} fusion(bf16[1,7168,256]{2,1,0:T(8,128)(2,1)} %param.17, f32[192,256]{1,0:T(8,128)S(1)} %fusion.5, bf16[1,7168,256]{2,1,0:T(8,128)(2,1)} %param.18, bf16[192,14336]{1,0:T(8,128)(2,1)} %all-gather.5.cloned.1.call-done, f32[192,256]{1,0:T(8,128)S(1)} %fusion.15), kind=kOutput, calls=%fused_computation.20 | convolution fusion | flops 1409777664 | bytes 15990784 | tf_op jit(solution)/shard_map/dot_general | solution.py:113
  155.4 6.7 %fusion = bf16[192,7168]{1,0:T(8,128)(2,1)} fusion(f32[192,7168]{1,0:T(8,128)} %fusion.13, bf16[1,7168,256]{2,1,0:T(8,128)(2,1)} %param.18, f32[192,256]{1,0:T(8,128)S(1)} %fusion.5, f32[192,256]{1,0:T(8,128)S(1)} %fusion.15), kind=kOutput, calls=%fused_computation.1 | convolution fusion | flops 707690496 | bytes 12320768 | tf_op jit(solution)/shard_map/dot_general | solution.py:114
  162.1 18.7 %reduce-scatter.3.cloned.1.call-done = bf16[24,7168]{1,0:T(8,128)(2,1)} async-done(((bf16[192,7168]{1,0:T(8,128)(2,1)}), bf16[24,7168]{1,0:T(8,128)(2,1)}) %reduce-scatter.3.cloned.1.call-update) | async-done | bytes 344080 | tf_op jit(solution)/shard_map/reduce_scatter | solution.py:78
  180.8 2.0 reshape.66
  182.7 6.3 %all-to-all-start.1 = ((bf16[8,3,7168]{2,1,0:T(4,128)(2,1)}), bf16[8,3,7168]{2,1,0:T(4,128)(2,1)S(1)}, u32[]{:S(2)}, u32[]{:S(2)}) async-start(bf16[8,3,7168]{2,1,0:T(4,128)(2,1)} %reshape.66), calls=%async_computation.2 | async-start | bytes 917504 | tf_op jit(solution)/shard_map/all_to_all | solution.py:81
  189.0 0.1 copy.19
  189.1 0.1 mul.74
  189.2 0.1 mul.67
  189.3 0.3 fusion.68
  189.6 37.7 %reduce-scatter.5.cloned.1.call-done = bf16[24,7168]{1,0:T(8,128)(2,1)} async-done(((bf16[192,7168]{1,0:T(8,128)(2,1)}), bf16[24,7168]{1,0:T(8,128)(2,1)}) %reduce-scatter.5.cloned.1.call-update) | async-done | bytes 344080 | tf_op jit(solution)/shard_map/reduce_scatter | solution.py:78
  227.3 2.0 reshape.71
  229.2 6.6 %all-to-all-start.3 = ((bf16[8,3,7168]{2,1,0:T(4,128)(2,1)}), bf16[8,3,7168]{2,1,0:T(4,128)(2,1)S(1)}, u32[]{:S(2)}, u32[]{:S(2)}) async-start(bf16[8,3,7168]{2,1,0:T(4,128)(2,1)} %reshape.71), calls=%async_computation.5 | async-start | bytes 917504 | tf_op jit(solution)/shard_map/all_to_all | solution.py:81
  235.8 0.3 fusion.71
  236.1 0.3 reshape.67
  236.4 0.3 fusion.4
  236.7 5.2 %collective-permute-start = (bf16[1,8,7168]{2,1,0:T(8,128)(2,1)S(1)}, bf16[1,8,7168]{2,1,0:T(8,128)(2,1)S(1)}, u32[]{:S(2)}, u32[]{:S(2)}) collective-permute-start(bf16[1,8,7168]{2,1,0:T(8,128)(2,1)S(1)} %fusion.4), channel_id=1, source_target_pairs={{192,0},{0,64},{64,128},{128,192},{193,1},{1,65},{65,129},{129,193... | collective-permute-start | bytes 344072 | tf_op jit(solution)/shard_map/ppermute | solution.py:12
  241.9 2.3 all-to-all-done.3
  244.2 0.3 reshape.72
  244.5 0.3 fusion.3
  244.8 6.4 %collective-permute-start.1 = (bf16[1,8,7168]{2,1,0:T(8,128)(2,1)S(1)}, bf16[1,8,7168]{2,1,0:T(8,128)(2,1)S(1)}, u32[]{:S(2)}, u32[]{:S(2)}) collective-permute-start(bf16[1,8,7168]{2,1,0:T(8,128)(2,1)S(1)} %fusion.3), channel_id=1, source_target_pairs={{64,0},{128,64},{192,128},{0,192},{65,1},{129,65},{193,129},{1,193... | collective-permute-start | bytes 344072 | tf_op jit(solution)/shard_map/ppermute | solution.py:12
  251.2 3.0 %collective-permute-done.1 = bf16[1,8,7168]{2,1,0:T(8,128)(2,1)S(1)} collective-permute-done((bf16[1,8,7168]{2,1,0:T(8,128)(2,1)S(1)}, bf16[1,8,7168]{2,1,0:T(8,128)(2,1)S(1)}, u32[]{:S(2)}, u32[]{:S(2)}) %collective-permute-start.1) | collective-permute-done | bytes 114720 | tf_op jit(solution)/shard_map/ppermute | solution.py:12
  254.2 0.6 copy.22
  254.8 0.6 copy.23
  (31 shorter events, 0.6 us)
Async XLA Ops:
  7.2 22.2 %copy-start = (bf16[1,8,7168]{2,1,0:T(8,128)(2,1)S(1)}, bf16[1,8,7168]{2,1,0:T(8,128)(2,1)}, u32[]{:S(2)}) copy-start(bf16[1,8,7168]{2,1,0:T(8,128)(2,1)} %param.13) | copy-start | bytes 344068
  7.2 22.7 %copy-start.4 = (bf16[1,8,7168]{2,1,0:T(8,128)(2,1)S(1)}, bf16[1,8,7168]{2,1,0:T(8,128)(2,1)}, u32[]{:S(2)}) copy-start(bf16[1,8,7168]{2,1,0:T(8,128)(2,1)} %param.14) | copy-start | bytes 344068
  7.2 61.3 %all-gather.3.cloned.1.call-start = ((), (), s32[]{:S(2)}) async-start(), calls=%async_computation.6 | async-start | bytes 3096576 | tf_op jit(solution)/shard_map/all_gather | solution.py:75
  27.9 110.7 %all-gather.5.cloned.1.call-start = ((), (), s32[]{:S(2)}) async-start(), calls=%async_computation.8 | async-start | bytes 6193152 | tf_op jit(solution)/shard_map/all_gather | solution.py:75
  48.9 131.8 %reduce-scatter.3.cloned.1.call-start = ((), (), s32[]{:S(2)}) async-start(), calls=%async_computation.7 | async-start | bytes 3096576 | tf_op jit(solution)/shard_map/reduce_scatter | solution.py:78
  68.5 3.9 %copy-start.1 = (bf16[192,7168]{1,0:T(8,128)(2,1)S(1)}, bf16[192,7168]{1,0:T(8,128)(2,1)}, u32[]{:S(2)}) copy-start(bf16[192,7168]{1,0:T(8,128)(2,1)} %all-gather.3.cloned.1.call-done) | copy-start | bytes 8257540
  80.3 146.9 %reduce-scatter.5.cloned.1.call-start = ((), (), s32[]{:S(2)}) async-start(), calls=%async_computation.9 | async-start | bytes 3096576 | tf_op jit(solution)/shard_map/reduce_scatter | solution.py:78
  138.6 3.9 %copy-start.2 = (bf16[1,256,7168]{2,1,0:T(8,128)(2,1)S(1)}, bf16[1,256,7168]{2,1,0:T(8,128)(2,1)}, u32[]{:S(2)}) copy-start(bf16[1,256,7168]{2,1,0:T(8,128)(2,1)} %param.19) | copy-start | bytes 11010052
  162.1 26.9 %copy-start.5 = (f32[1,8,2]{1,2,0:T(2,128)S(1)}, f32[1,8,2]{1,2,0:T(2,128)}, u32[]{:S(2)}) copy-start(f32[1,8,2]{1,2,0:T(2,128)} %param.16) | copy-start | bytes 196
  162.1 27.1 %copy-start.6 = (f32[1,8,2]{1,2,0:T(2,128)S(1)}, f32[1,8,2]{1,2,0:T(2,128)}, u32[]{:S(2)}) copy-start(f32[1,8,2]{1,2,0:T(2,128)} %param.12) | copy-start | bytes 196
  162.1 74.3 %copy-start.3 = (bf16[1,8,7168]{2,1,0:T(8,128)(2,1)S(1)}, bf16[1,8,7168]{2,1,0:T(8,128)(2,1)}, u32[]{:S(2)}) copy-start(bf16[1,8,7168]{2,1,0:T(8,128)(2,1)} %param.10) | copy-start | bytes 344068
  182.7 46.5 %all-to-all-start.1 = ((bf16[8,3,7168]{2,1,0:T(4,128)(2,1)}), bf16[8,3,7168]{2,1,0:T(4,128)(2,1)S(1)}, u32[]{:S(2)}, u32[]{:S(2)}) async-start(bf16[8,3,7168]{2,1,0:T(4,128)(2,1)} %reshape.66), calls=%async_computation.2 | async-start | bytes 917504 | tf_op jit(solution)/shard_map/all_to_all | solution.py:81
  229.2 15.0 %all-to-all-start.3 = ((bf16[8,3,7168]{2,1,0:T(4,128)(2,1)}), bf16[8,3,7168]{2,1,0:T(4,128)(2,1)S(1)}, u32[]{:S(2)}, u32[]{:S(2)}) async-start(bf16[8,3,7168]{2,1,0:T(4,128)(2,1)} %reshape.71), calls=%async_computation.5 | async-start | bytes 917504 | tf_op jit(solution)/shard_map/all_to_all | solution.py:81
  236.7 14.5 %collective-permute-start = (bf16[1,8,7168]{2,1,0:T(8,128)(2,1)S(1)}, bf16[1,8,7168]{2,1,0:T(8,128)(2,1)S(1)}, u32[]{:S(2)}, u32[]{:S(2)}) collective-permute-start(bf16[1,8,7168]{2,1,0:T(8,128)(2,1)S(1)} %fusion.4), channel_id=1, source_target_pairs={{192,0},{0,64},{64,128},{128,192},{193,1},{1,65},{65,129},{129,193... | collective-permute-start | bytes 344072 | tf_op jit(solution)/shard_map/ppermute | solution.py:12
  244.8 9.4 %collective-permute-start.1 = (bf16[1,8,7168]{2,1,0:T(8,128)(2,1)S(1)}, bf16[1,8,7168]{2,1,0:T(8,128)(2,1)S(1)}, u32[]{:S(2)}, u32[]{:S(2)}) collective-permute-start(bf16[1,8,7168]{2,1,0:T(8,128)(2,1)S(1)} %fusion.3), channel_id=1, source_target_pairs={{64,0},{128,64},{192,128},{0,192},{65,1},{129,65},{193,129},{1,193... | collective-permute-start | bytes 344072 | tf_op jit(solution)/shard_map/ppermute | solution.py:12
Sparse Core Ops, SparseCore 0:
  28.0 40.4 all-gather.2
  70.3 68.2 all-gather.4
  141.1 39.5 reduce-scatter.2
  183.2 44.0 reduce-scatter.4
